TPU v7x, 128 devices: a whole 4x4x4 slice. The times are simulated.
128 devices in a mesh: tgt: 16 (over z, x), src: 8 (over y, core).
Axes of the slice: x: 4, y: 4, z: 4, core: 2. Of those that a mesh axis runs over, the one named last changes fastest.
Arguments:
- points: bfloat16 [262144, 256], P(('tgt', 'src')), may hold values from -0.4 to 0.4
- weights: bfloat16 [262144, 64], P(('tgt', 'src')), may hold values from -6 to 6
- near_list: int32 [2048, 16], P(('tgt', 'src')), may hold values from -1 to 127, as said below
- far_list: int32 [2048, 3, 8], P('tgt', None, 'src'), may hold values from -1 to 63, as said below
- skel_index: int32 [896, 256], P(('tgt', 'src')), may hold values from 0 to 2047, as said below
- equiv_weights: bfloat16 [896, 256, 64], P(('tgt', 'src')), may hold values from -6 to 6
Outputs:
- potential: float32 [262144, 64], P(('tgt', 'src'))
Inputs may be any that keep to these rules, and one draw needn't show every extreme that they name: `near_list`: row b lists blocks of b's group of 128 blocks by their index within the group: first b itself, then distinct other blocks; after a row's live entries all are -1; every row has 4 or more live entries. `far_list`: entry [b, l, c] is -1 or a level-l node owned by a device of src index c, numbered as the owner's tgt index times (16 // (4 * 2 ** l)) plus the node's number among the owner's level-l nodes. `skel_index`: Level-l nodes of a device cover 4 * 128 * 2 ** l consecutive points of that device each, in order; a node's 256 entries are increasing indices of the device's points inside the node.
All inputs are finite; a program needn't handle non-finite values.
Results may differ from a plain program's by a relative error of at most 0.0023.
Values may be sent and summed in bfloat16 or wider, within the bound.
No kernel may reach another device: no remote copies, remote signals or barrier semaphores. Data moves between devices by JAX's collectives and lax.ppermute only.
A program may use at most 192 MiB of HBM per device.

v0:
```python
import jax
import jax.numpy as jnp
from jax import lax
from jax.sharding import PartitionSpec as P

E = 256
WCOL = 64
BLK = 128
RANK = 256
NEAR = 16
LEVELS = 3
kernel_rate = 2.0


def square_norms(values):
    return jnp.sum(jnp.square(values.astype(jnp.float32)), axis=-1)


def tile_kernel(targets, target_norms, sources, source_norms, live_mask):
    dot_terms = jnp.einsum("bie,bse->bis", targets, sources, preferred_element_type=jnp.float32)
    sq_dist = target_norms[:, :, None] + source_norms[:, None, :] - 2.0 * dot_terms
    return jnp.where(live_mask[:, None, :], jnp.exp(-kernel_rate * sq_dist), 0.0).astype(
        jnp.bfloat16
    )


def apply_tile(kernel, source_weights):
    return jnp.einsum("bis,bsw->biw", kernel, source_weights, preferred_element_type=jnp.float32)


def shards(points, weights, near_list, far_list, skel_index, equiv_weights):
    point_dev = points.shape[0]
    blk_dev = point_dev // BLK
    src_size = lax.axis_size("src")
    src_index = lax.axis_index("src")
    group_blocks = src_size * blk_dev
    node_dev = skel_index.shape[0]
    level_nodes = [blk_dev // (4 * 2**tree_level) for tree_level in range(LEVELS)]
    level_start = [sum(level_nodes[:tree_level]) for tree_level in range(LEVELS)]
    group_pts, group_wts = (
        lax.all_gather(points, "src", axis=0, tiled=True),
        lax.all_gather(weights, "src", axis=0, tiled=True),
    )
    tgt_blocks = group_pts.reshape(group_blocks, BLK, E)
    tgt_norms = square_norms(group_pts).reshape(group_blocks, BLK)
    wt_blocks = group_wts.reshape(group_blocks, BLK, WCOL)
    skel_pts = jnp.take(points, skel_index.reshape(-1), axis=0).reshape(node_dev, RANK, E)
    panels = []
    for tree_level in range(LEVELS):
        first_node = level_start[tree_level]
        last_node = first_node + level_nodes[tree_level]
        lvl_pts, lvl_wts = (
            lax.all_gather(skel_pts[first_node:last_node], "tgt", axis=0, tiled=True),
            lax.all_gather(equiv_weights[first_node:last_node], "tgt", axis=0, tiled=True),
        )
        panels.append((lvl_pts, square_norms(lvl_pts), lvl_wts, level_nodes[tree_level], 0))
    own_blocks = points.reshape(blk_dev, BLK, E)
    own_norms = lax.dynamic_slice_in_dim(tgt_norms, src_index * blk_dev, blk_dev, 0)
    near_live = near_list >= 0
    near_index = jnp.where(near_live, near_list, 0)
    sources = tgt_blocks[near_index].reshape(blk_dev, NEAR * BLK, E)
    source_norms = tgt_norms[near_index].reshape(blk_dev, NEAR * BLK)
    source_wts = wt_blocks[near_index].reshape(blk_dev, NEAR * BLK, WCOL)
    kernel = tile_kernel(
        own_blocks, own_norms, sources, source_norms, jnp.repeat(near_live, BLK, axis=1)
    )
    own_near = apply_tile(kernel, source_wts).reshape(point_dev, WCOL)
    row_count = src_size * point_dev
    block_count = row_count // BLK
    far_total = jnp.zeros((block_count, BLK, WCOL), jnp.float32)
    for tree_level in range(LEVELS):
        panel_pts, panel_norms, panel_wts, stride_rows, offset_rows = panels[tree_level]
        level_count = level_nodes[tree_level]
        far_entry = far_list[:, tree_level, 0]
        far_live = far_entry >= 0
        far_entry = jnp.where(far_live, far_entry, 0)
        panel_rows = far_entry // level_count * stride_rows + offset_rows + far_entry % level_count
        kernel = tile_kernel(
            tgt_blocks,
            tgt_norms,
            panel_pts[panel_rows],
            panel_norms[panel_rows],
            jnp.broadcast_to(far_live[:, None], (block_count, RANK)),
        )
        far_total = far_total + apply_tile(kernel, panel_wts[panel_rows])
    whole_term = lax.psum(far_total.reshape(row_count, WCOL), "src")
    mine_term = lax.dynamic_slice_in_dim(whole_term, src_index * point_dev, point_dev, 0)
    mine_term = mine_term + own_near
    return mine_term


def solution(mesh):
    in_specs = (
        P(("tgt", "src"), None),
        P(("tgt", "src"), None),
        P(("tgt", "src"), None),
        P("tgt", None, "src"),
        P(("tgt", "src"), None),
        P(("tgt", "src"), None, None),
    )
    out_specs = P(("tgt", "src"), None)
    return jax.shard_map(shards, mesh=mesh, in_specs=in_specs, out_specs=out_specs, check_vma=False)
```

profile of v0, /device:TPU:0, one launch (start us, length us, event | category | flops | bytes accessed | tf_op | source)
XLA Modules:
  0.0 471.0 jit_solution(658145759099932878)
XLA Ops:
  10.4 5.5 %gather_fusion = bf16[1792,256]{1,0:T(8,128)(2,1)S(1)} fusion(bf16[2048,256]{1,0:T(8,128)(2,1)} %param.6, s32[2048]{0:T(1024)S(1)} %pad_clamp_fusion), kind=kCustom, calls=%fused_computation | custom fusion | bytes 1842176 | tf_op jit(solution)/shard_map/jit(_take)/gather | solution.py:47
  20.4 26.1 %all_gather.30 = bf16[16,256,64]{1,2,0:T(8,128)(2,1)S(1)} all-gather(bf16[1,256,64]{1,2,0:T(8,128)(2,1)S(1)} %slice-done), channel_id=1, replica_groups=mesh['tgt'=16,'src'=8] {'tgt'}, dimensions={0}, use_global_device_ids=true | all-gather | bytes 557056 | tf_op jit(solution)/shard_map/all_gather | solution.py:54
  49.3 5.6 %all-gather.17.cloned.1.call-done = bf16[32,256,64]{1,2,0:T(8,128)(2,1)} async-done(((bf16[2,256,64]{1,2,0:T(8,128)(2,1)}), bf16[32,256,64]{1,2,0:T(8,128)(2,1)}) %all-gather.17.cloned.1.call-update) | async-done | bytes 1048592 | tf_op jit(solution)/shard_map/all_gather | solution.py:54
  58.9 22.5 %all-gather.19.cloned.1.call-done = bf16[16384,64]{0,1:T(8,128)(2,1)} async-done(((bf16[2048,64]{0,1:T(8,128)(2,1)}), bf16[16384,64]{0,1:T(8,128)(2,1)}) %all-gather.19.cloned.1.call-update) | async-done | bytes 2097168 | tf_op jit(solution)/shard_map/all_gather | solution.py:42
  86.7 6.9 %copy.25 = bf16[256,128,64]{1,0,2:T(8,128)(2,1)} copy(bf16[256,128,64]{1,2,0:T(8,128)(2,1)} %gather_fusion.12) | data formatting | bytes 8388608 | tf_op jit(solution)/shard_map/gather | solution.py:63
  93.6 7.3 %reshape.311 = bf16[16,2048,64]{1,0,2:T(8,128)(2,1)} reshape(bf16[256,128,64]{1,0,2:T(8,128)(2,1)} %copy.25) | data formatting | bytes 8388608 | tf_op jit(solution)/shard_map/reshape | solution.py:63
  100.9 28.0 %all-gather.21.cloned.1.call-done = bf16[4096,256]{1,0:T(8,128)(2,1)} async-done(((bf16[256,256]{1,0:T(8,128)(2,1)}), bf16[4096,256]{1,0:T(8,128)(2,1)}) %all-gather.21.cloned.1.call-update) | async-done | bytes 2097168 | tf_op jit(solution)/shard_map/all_gather | solution.py:53
  128.9 10.0 %gather_fusion.8 = bf16[128,256,256]{2,1,0:T(8,128)(2,1)} fusion(bf16[16,256,256]{2,1,0:T(8,128)(2,1)} %bitcast.126, s32[1024]{0:T(1024)S(1)} %pad_clamp_fusion.2), kind=kCustom, calls=%fused_computation.8 | custom fusion | bytes 33554944 | tf_op jit(solution)/shard_map/gather | solution.py:81
  140.3 34.9 %all-gather.13.cloned.1.call-done = bf16[64,256,64]{1,2,0:T(8,128)(2,1)} async-done(((bf16[4,256,64]{1,2,0:T(8,128)(2,1)}), bf16[64,256,64]{1,2,0:T(8,128)(2,1)}) %all-gather.13.cloned.1.call-update) | async-done | bytes 2097168 | tf_op jit(solution)/shard_map/all_gather | solution.py:54
  179.6 48.4 %all-gather.15.cloned.1.call-done = bf16[32,256,256]{2,1,0:T(8,128)(2,1)} async-done(((bf16[2,256,256]{2,1,0:T(8,128)(2,1)}), bf16[32,256,256]{2,1,0:T(8,128)(2,1)}) %all-gather.15.cloned.1.call-update) | async-done | bytes 4194320 | tf_op jit(solution)/shard_map/all_gather | solution.py:53
  232.1 11.1 %gather_fusion.5 = bf16[128,256,256]{2,1,0:T(8,128)(2,1)} fusion(bf16[32,256,256]{2,1,0:T(8,128)(2,1)} %all-gather.15.cloned.1.call-done, s32[1024]{0:T(1024)S(1)} %pad_clamp_fusion.3), kind=kCustom, calls=%fused_computation.5 | custom fusion | bytes 33554944 | tf_op jit(solution)/shard_map/gather | solution.py:81
  243.2 35.7 %all-gather.9.cloned.1.call-done = bf16[16384,256]{1,0:T(8,128)(2,1)} async-done(((bf16[2048,256]{1,0:T(8,128)(2,1)}), bf16[16384,256]{1,0:T(8,128)(2,1)}) %all-gather.9.cloned.1.call-update) | async-done | bytes 8388624 | tf_op jit(solution)/shard_map/all_gather | solution.py:41
  278.8 5.2 %multiply_reduce_fusion.1 = f32[16384]{0:T(1024)S(1)} fusion(bf16[16384,256]{1,0:T(8,128)(2,1)} %all-gather.9.cloned.1.call-done), kind=kLoop, calls=%fused_computation.34 | loop fusion | flops 12566528 | bytes 8454144 | tf_op jit(solution)/shard_map/reduce_sum | solution.py:16
  284.8 12.8 %gather_fusion.11 = bf16[256,128,256]{2,1,0:T(8,128)(2,1)} fusion(bf16[128,128,256]{2,1,0:T(8,128)(2,1)} %bitcast.128, s32[1024]{0:T(1024)S(1)} %pad_clamp_fusion.1), kind=kCustom, calls=%fused_computation.11 | custom fusion | bytes 33555456 | tf_op jit(solution)/shard_map/gather | solution.py:61
  297.6 14.1 %fusion.16 = f32[128,128,64]{1,2,0:T(8,128)} fusion(bf16[128,256,64]{1,2,0:T(8,128)(2,1)} %gather_fusion.9, bf16[128,256,256]{2,1,0:T(8,128)(2,1)} %gather_fusion.8, bf16[128,128,256]{2,1,0:T(8,128)(2,1)} %bitcast.129, f32[128,256]{1,0:T(8,128)S(1)} %gather_fusion.7, f32[128,128]{1,0:T(8,128)S(1)} %bitcast.135, pred[128]{0:T(512)(128)(4,1)S(1)} %get-tuple-element.6), kind=kOutput, calls=%fused_computation.35 | convolution fusion | flops 2709520384 | bytes 33751168 | tf_op jit(solution)/shard_map/bis,bsw->biw/dot_general | solution.py:28
  311.7 14.3 %fusion.17 = f32[128,128,64]{1,2,0:T(8,128)} fusion(bf16[128,256,64]{1,2,0:T(8,128)(2,1)} %gather_fusion.6, bf16[128,256,256]{2,1,0:T(8,128)(2,1)} %gather_fusion.5, bf16[128,128,256]{2,1,0:T(8,128)(2,1)} %bitcast.130, f32[128,256]{1,0:T(8,128)S(1)} %gather_fusion.4, f32[128,128]{1,0:T(8,128)S(1)} %bitcast.136, pred[128]{0:T(512)(128)(4,1)S(1)} %get-tuple-element.7), kind=kOutput, calls=%fused_computation.36 | convolution fusion | flops 2709520384 | bytes 33751168 | tf_op jit(solution)/shard_map/bis,bsw->biw/dot_general | solution.py:28
  326.0 26.1 %all-gather.11.cloned.1.call-done = bf16[64,256,256]{2,1,0:T(8,128)(2,1)} async-done(((bf16[4,256,256]{2,1,0:T(8,128)(2,1)}), bf16[64,256,256]{2,1,0:T(8,128)(2,1)}) %all-gather.11.cloned.1.call-update) | async-done | bytes 8388624 | tf_op jit(solution)/shard_map/all_gather | solution.py:53
  352.1 5.6 %multiply_reduce_fusion = f32[64,256]{1,0:T(8,128)S(1)} fusion(bf16[64,256,256]{2,1,0:T(8,128)(2,1)} %all-gather.11.cloned.1.call-done), kind=kLoop, calls=%fused_computation.33 | loop fusion | flops 12566528 | bytes 8454144 | tf_op jit(solution)/shard_map/reduce_sum | solution.py:16
  358.5 11.6 %gather_fusion.2 = bf16[128,256,256]{2,1,0:T(8,128)(2,1)} fusion(bf16[64,256,256]{2,1,0:T(8,128)(2,1)} %all-gather.11.cloned.1.call-done, s32[1024]{0:T(1024)S(1)} %pad_clamp_fusion.4), kind=kCustom, calls=%fused_computation.2 | custom fusion | bytes 33554944 | tf_op jit(solution)/shard_map/gather | solution.py:81
  370.1 15.5 %add_bitcast_fusion = f32[128,8,8,128]{3,2,1,0:T(8,128)} fusion(f32[128,128,64]{1,2,0:T(8,128)} %fusion.16, f32[128,128,64]{1,2,0:T(8,128)} %fusion.17, bf16[128,256,64]{1,2,0:T(8,128)(2,1)} %gather_fusion.3, bf16[128,256,256]{2,1,0:T(8,128)(2,1)} %gather_fusion.2, bf16[128,128,256]{2,1,0:T(8,128)(2,1)} %bitcast.131, f32[128,256]{1,0:T(8,128)S(1)} %gather_fusion.1, ...), kind=kOutput, calls=%fused_computation.62 | convolution fusion | flops 2711617536 | bytes 42139776 | tf_op jit(solution)/shard_map/bis,bsw->biw/dot_general | solution.py:28
  385.7 4.5 copy.47
  390.2 12.0 %fusion.87 = bf16[16,128,2048]{1,2,0:T(8,128)(2,1)S(1)} fusion(f32[16,2048]{1,0:T(8,128)S(1)} %add.225, f32[16,128]{1,0:T(8,128)S(1)} %constant_dynamic-slice_fusion, pred[16,2048]{1,0:T(8,128)(4,1)S(1)} %bitcast.143, bf16[16,2048,256]{2,1,0:T(8,128)(2,1)} %bitcast.138, bf16[16,128,256]{2,1,0:T(8,128)(2,1)S(1)} %bitcast.132), kind=kOutput, calls=%fused_computation.17.clone.clone.clone.clone.1 | convolution fusion | flops 2172649472 | bytes 26386432 | tf_op jit(solution)/shard_map/bie,bse->bis/dot_general | solution.py:20
  402.2 5.0 %fusion.43 = f32[16,8,8,128]{3,2,1,0:T(8,128)S(1)} fusion(bf16[16,2048,64]{1,0,2:T(8,128)(2,1)S(1)} %copy-done.2, bf16[16,128,2048]{1,2,0:T(8,128)(2,1)S(1)} %fusion.87), kind=kOutput, calls=%fused_computation.65 | convolution fusion | flops 536870912 | bytes 13107200 | tf_op jit(solution)/shard_map/bis,bsw->biw/dot_general | solution.py:28
  407.2 55.1 %all-reduce.2.cloned.1.call-done = f32[16384,64]{0,1:T(8,128)} async-done(((f32[16384,64]{0,1:T(8,128)}), f32[16384,64]{0,1:T(8,128)}) %all-reduce.2.cloned.1.call-update) | async-done | bytes 4194320 | tf_op jit(solution)/shard_map/psum | solution.py:86
  (66 shorter events, 33.5 us)
Async XLA Ops:
  6.5 10.5 %copy-start.3 = (bf16[7,256,64]{1,2,0:T(8,128)(2,1)S(1)}, bf16[7,256,64]{1,2,0:T(8,128)(2,1)}, u32[]{:S(2)}) copy-start(bf16[7,256,64]{1,2,0:T(8,128)(2,1)} %param.11) | copy-start | bytes 688132
  6.5 13.8 %slice-start = ((bf16[7,256,64]{1,2,0:T(8,128)(2,1)}), bf16[1,256,64]{1,2,0:T(8,128)(2,1)S(1)}, s32[]{:S(2)}) async-start(bf16[7,256,64]{1,2,0:T(8,128)(2,1)} %param.11), calls=%async_computation.8 | async-start | bytes 65536 | tf_op jit(solution)/shard_map/slice | solution.py:54
  6.5 13.5 %copy-start.4 = (s32[16,16]{1,0:T(8,128)S(1)}, s32[16,16]{1,0:T(8,128)}, u32[]{:S(2)}) copy-start(s32[16,16]{1,0:T(8,128)} %param.8) | copy-start | bytes 3076
  6.5 13.8 %copy-start.5 = (s32[128,3,1]{0,2,1:T(1,128)S(1)}, s32[128,3,1]{0,2,1:T(1,128)}, u32[]{:S(2)}) copy-start(s32[128,3,1]{0,2,1:T(1,128)} %param.9) | copy-start | bytes 4612
  6.5 48.4 %all-gather.17.cloned.1.call-start = ((), (), s32[]{:S(2)}) async-start(), calls=%async_computation.4 | async-start | bytes 1114112 | tf_op jit(solution)/shard_map/all_gather | solution.py:54
  8.2 73.2 %all-gather.19.cloned.1.call-start = ((), (), s32[]{:S(2)}) async-start(), calls=%async_computation.6 | async-start | bytes 2359296 | tf_op jit(solution)/shard_map/all_gather | solution.py:42
  8.9 120.0 %all-gather.21.cloned.1.call-start = ((), (), s32[]{:S(2)}) async-start(), calls=%async_computation.7 | async-start | bytes 2228224 | tf_op jit(solution)/shard_map/all_gather | solution.py:53
  17.0 158.2 %all-gather.13.cloned.1.call-start = ((), (), s32[]{:S(2)}) async-start(), calls=%async_computation.2 | async-start | bytes 2228224 | tf_op jit(solution)/shard_map/all_gather | solution.py:54
  17.7 210.3 %all-gather.15.cloned.1.call-start = ((), (), s32[]{:S(2)}) async-start(), calls=%async_computation.3 | async-start | bytes 4456448 | tf_op jit(solution)/shard_map/all_gather | solution.py:53
  18.6 260.3 %all-gather.9.cloned.1.call-start = ((), (), s32[]{:S(2)}) async-start(), calls=%async_computation | async-start | bytes 9437184 | tf_op jit(solution)/shard_map/all_gather | solution.py:41
  19.1 333.0 %all-gather.11.cloned.1.call-start = ((), (), s32[]{:S(2)}) async-start(), calls=%async_computation.1 | async-start | bytes 8912896 | tf_op jit(solution)/shard_map/all_gather | solution.py:53
  20.0 442.3 %all-reduce.2.cloned.1.call-start = ((), (), s32[]{:S(2)}) async-start(), calls=%async_computation.5 | async-start | bytes 8388608 | tf_op jit(solution)/shard_map/psum | solution.py:86
  128.9 10.0 %copy-start = (bf16[4096,256]{1,0:T(8,128)(2,1)S(1)}, bf16[4096,256]{1,0:T(8,128)(2,1)}, u32[]{:S(2)}) copy-start(bf16[4096,256]{1,0:T(8,128)(2,1)} %all-gather.21.cloned.1.call-done) | copy-start | bytes 6291460
  385.7 4.5 copy-start.1
  390.2 12.0 %copy-start.2 = (bf16[16,2048,64]{1,0,2:T(8,128)(2,1)S(1)}, bf16[16,2048,64]{1,0,2:T(8,128)(2,1)}, u32[]{:S(2)}) copy-start(bf16[16,2048,64]{1,0,2:T(8,128)(2,1)} %reshape.311) | copy-start | bytes 12582916
Sparse Core Ops, SparseCore 0:
  9.5 45.4 all-gather.16
  56.6 24.7 all-gather.18
  83.6 45.3 all-gather.20
  130.9 44.2 all-gather.12
  177.2 50.7 all-gather.14
  229.6 49.2 all-gather.8
  281.0 71.0 all-gather.10
  390.3 71.9 all-reduce.1
where the time goes:
time: 472 us; the launch traced here: 471 us
  waiting for transfers between devices  257 us (54%)
  local copies, waits for them, and re-layouts  95.4 us (20%)
  matrix products  60.9 us (13%)
  blocking collectives  26.1 us (6%)
  other arithmetic  17.1 us (4%)
  between operations  13.7 us (3%)
    all_gather x3, waiting for transfers between devices, shards(): lax.all_gather(skel_pts[first_node:last_node], 'tgt', axis=0, tiled=True)  102 us
    psum x1, waiting for transfers between devices, shards(): whole_term = lax.psum(far_total.reshape(row_count, WCOL), 'src')  55.1 us
    dot_general x4, matrix products, apply_tile(): jnp.einsum('bis,bsw->biw', kernel, source_weights, preferred_element_type...  49 us
    all_gather x2, waiting for transfers between devices, shards(): lax.all_gather(equiv_weights[first_node:last_node], 'tgt', axis=0, tiled=...  40.5 us
    all_gather x1, waiting for transfers between devices, shards(): lax.all_gather(points, 'src', axis=0, tiled=True)  35.7 us
    gather x3, local copies, waits for them, and re-layouts, shards(): panel_pts[panel_rows]  32.8 us
    all_gather x1, blocking collectives, shards(): lax.all_gather(equiv_weights[first_node:last_node], 'tgt', axis=0, tiled=...  26.1 us
    all_gather x1, waiting for transfers between devices, shards(): lax.all_gather(weights, 'src', axis=0, tiled=True)  22.5 us
  transfers between devices with their start and end apart: 8, of which 8 were waited for; matrix products, arithmetic and copies ran while one was open for 28% of the time, Pallas kernels for 0%

commit v1 on v0

--- a/solution.py
+++ b/solution.py
@@ -83,7 +83,7 @@
             jnp.broadcast_to(far_live[:, None], (block_count, RANK)),
         )
         far_total = far_total + apply_tile(kernel, panel_wts[panel_rows])
-    whole_term = lax.psum(far_total.reshape(row_count, WCOL), "src")
+    whole_term = jnp.sum(lax.all_gather(far_total.reshape(row_count, WCOL), "src"), axis=0)
     mine_term = lax.dynamic_slice_in_dim(whole_term, src_index * point_dev, point_dev, 0)
     mine_term = mine_term + own_near
     return mine_term

time: 472 us -> 550 us (1.17)
  waiting for transfers between devices: 257 us -> 312 us
  other arithmetic: 17.1 us -> 31.1 us
  local copies, waits for them, and re-layouts: 95.4 us -> 104 us
    all_gather x0 -> x1, waiting for transfers between devices: none -> 104 us  [shards(): lax.all_gather(far_total.reshape(row_count, WCOL), 'src')]
    psum x1 -> x0, waiting for transfers between devices: 55.1 us -> none  [shards(): whole_term = lax.psum(far_total.reshape(row_count, WCOL), 'src')]
    all_gather x3, waiting for transfers between devices: 102 us -> 131 us  [shards(): lax.all_gather(skel_pts[first_node:last_node], 'tgt', axis=0, tiled=True)]
    all_gather x1, waiting for transfers between devices: 22.5 us -> 0.02 us  [shards(): lax.all_gather(weights, 'src', axis=0, tiled=True)]
    reduce_sum x0 -> x1, other arithmetic: none -> 14 us  [shards(): jnp.sum(lax.all_gather(far_total.reshape(row_count, WCOL), 'src'), axis=0)]
    add x0 -> x1, local copies, waits for them, and re-layouts: none -> 6.56 us  [shards(): far_total = far_total + apply_tile(kernel, panel_wts[panel_rows])]
  transfers between devices with their start and end apart: 8 -> 8, of which waited for: 8 -> 7; matrix products, arithmetic and copies ran while one was open for 28% -> 33% of each run, Pallas kernels for 0% -> 0%
where the time goes in v1:
time: 550 us; the launch traced here: 548 us
  waiting for transfers between devices  312 us (57%)
  local copies, waits for them, and re-layouts  104 us (19%)
  matrix products  61.3 us (11%)
  other arithmetic  31.1 us (6%)
  blocking collectives  26.1 us (5%)
  between operations  13.7 us (2%)
    all_gather x3, waiting for transfers between devices, shards(): lax.all_gather(skel_pts[first_node:last_node], 'tgt', axis=0, tiled=True)  131 us
    all_gather x1, waiting for transfers between devices, shards(): lax.all_gather(far_total.reshape(row_count, WCOL), 'src')  104 us
    dot_general x4, matrix products, apply_tile(): jnp.einsum('bis,bsw->biw', kernel, source_weights, preferred_element_type...  49.1 us
    all_gather x2, waiting for transfers between devices, shards(): lax.all_gather(equiv_weights[first_node:last_node], 'tgt', axis=0, tiled=...  40.7 us
    all_gather x1, waiting for transfers between devices, shards(): lax.all_gather(points, 'src', axis=0, tiled=True)  35.6 us
    gather x3, local copies, waits for them, and re-layouts, shards(): panel_pts[panel_rows]  33.2 us
    all_gather x1, blocking collectives, shards(): lax.all_gather(equiv_weights[first_node:last_node], 'tgt', axis=0, tiled=...  26.1 us
    reduce_sum x4, other arithmetic, square_norms(): return jnp.sum(jnp.square(values.astype(jnp.float32)), axis=-1)  14.8 us
  transfers between devices with their start and end apart: 8, of which 7 were waited for; matrix products, arithmetic and copies ran while one was open for 33% of the time, Pallas kernels for 0%

profile of v1, /device:TPU:0, one launch (start us, length us, event | category | flops | bytes accessed | tf_op | source)
XLA Modules:
  0.0 548.4 jit_solution(17445586517761421595)
XLA Ops:
  9.6 5.5 %gather_fusion = bf16[1792,256]{1,0:T(8,128)(2,1)S(1)} fusion(bf16[2048,256]{1,0:T(8,128)(2,1)} %param.6, s32[2048]{0:T(1024)S(1)} %pad_clamp_fusion), kind=kCustom, calls=%fused_computation | custom fusion | bytes 1842176 | tf_op jit(solution)/shard_map/jit(_take)/gather | solution.py:47
  20.1 26.1 %all_gather.33 = bf16[16,256,64]{1,2,0:T(8,128)(2,1)S(1)} all-gather(bf16[1,256,64]{1,2,0:T(8,128)(2,1)S(1)} %slice-done), channel_id=1, replica_groups=mesh['tgt'=16,'src'=8] {'tgt'}, dimensions={0}, use_global_device_ids=true | all-gather | bytes 557056 | tf_op jit(solution)/shard_map/all_gather | solution.py:54
  49.0 5.8 %all-gather.18.cloned.1.call-done = bf16[32,256,64]{1,2,0:T(8,128)(2,1)} async-done(((bf16[2,256,64]{1,2,0:T(8,128)(2,1)}), bf16[32,256,64]{1,2,0:T(8,128)(2,1)}) %all-gather.18.cloned.1.call-update) | async-done | bytes 1048592 | tf_op jit(solution)/shard_map/all_gather | solution.py:54
  58.8 42.6 %all-gather.24.cloned.1.call-done = bf16[4096,256]{1,0:T(8,128)(2,1)} async-done(((bf16[256,256]{1,0:T(8,128)(2,1)}), bf16[4096,256]{1,0:T(8,128)(2,1)}) %all-gather.24.cloned.1.call-update) | async-done | bytes 2097168 | tf_op jit(solution)/shard_map/all_gather | solution.py:53
  101.4 10.2 %gather_fusion.8 = bf16[128,256,256]{2,1,0:T(8,128)(2,1)} fusion(bf16[16,256,256]{2,1,0:T(8,128)(2,1)} %bitcast.123, s32[1024]{0:T(1024)S(1)} %pad_clamp_fusion.2), kind=kCustom, calls=%fused_computation.8 | custom fusion | bytes 33554944 | tf_op jit(solution)/shard_map/gather | solution.py:81
  113.0 34.8 %all-gather.14.cloned.1.call-done = bf16[64,256,64]{1,2,0:T(8,128)(2,1)} async-done(((bf16[4,256,64]{1,2,0:T(8,128)(2,1)}), bf16[64,256,64]{1,2,0:T(8,128)(2,1)}) %all-gather.14.cloned.1.call-update) | async-done | bytes 2097168 | tf_op jit(solution)/shard_map/all_gather | solution.py:54
  152.2 48.4 %all-gather.16.cloned.1.call-done = bf16[32,256,256]{2,1,0:T(8,128)(2,1)} async-done(((bf16[2,256,256]{2,1,0:T(8,128)(2,1)}), bf16[32,256,256]{2,1,0:T(8,128)(2,1)}) %all-gather.16.cloned.1.call-update) | async-done | bytes 4194320 | tf_op jit(solution)/shard_map/all_gather | solution.py:53
  204.7 11.1 %gather_fusion.5 = bf16[128,256,256]{2,1,0:T(8,128)(2,1)} fusion(bf16[32,256,256]{2,1,0:T(8,128)(2,1)} %all-gather.16.cloned.1.call-done, s32[1024]{0:T(1024)S(1)} %pad_clamp_fusion.3), kind=kCustom, calls=%fused_computation.5 | custom fusion | bytes 33554944 | tf_op jit(solution)/shard_map/gather | solution.py:81
  215.8 35.6 %all-gather.10.cloned.1.call-done = bf16[16384,256]{1,0:T(8,128)(2,1)} async-done(((bf16[2048,256]{1,0:T(8,128)(2,1)}), bf16[16384,256]{1,0:T(8,128)(2,1)}) %all-gather.10.cloned.1.call-update) | async-done | bytes 8388624 | tf_op jit(solution)/shard_map/all_gather | solution.py:41
  251.5 5.2 multiply_reduce_fusion.1
  256.7 14.3 %fusion.16 = f32[128,128,64]{1,2,0:T(8,128)} fusion(bf16[128,256,64]{1,2,0:T(8,128)(2,1)} %gather_fusion.9, bf16[128,256,256]{2,1,0:T(8,128)(2,1)} %gather_fusion.8, bf16[128,128,256]{2,1,0:T(8,128)(2,1)} %bitcast.125, f32[128,256]{1,0:T(8,128)S(1)} %gather_fusion.7, f32[128,128]{1,0:T(8,128)S(1)} %bitcast.130, pred[128]{0:T(512)(128)(4,1)S(1)} %get-tuple-element.6), kind=kOutput, calls=%fused_computation.35 | convolution fusion | flops 2709520384 | bytes 33751168 | tf_op jit(solution)/shard_map/bis,bsw->biw/dot_general | solution.py:28
  271.0 14.0 %fusion.17 = f32[128,128,64]{1,2,0:T(8,128)} fusion(bf16[128,256,64]{1,2,0:T(8,128)(2,1)} %gather_fusion.6, bf16[128,256,256]{2,1,0:T(8,128)(2,1)} %gather_fusion.5, bf16[128,128,256]{2,1,0:T(8,128)(2,1)} %bitcast.126, f32[128,256]{1,0:T(8,128)S(1)} %gather_fusion.4, f32[128,128]{1,0:T(8,128)S(1)} %bitcast.131, pred[128]{0:T(512)(128)(4,1)S(1)} %get-tuple-element.7), kind=kOutput, calls=%fused_computation.36 | convolution fusion | flops 2709520384 | bytes 33751168 | tf_op jit(solution)/shard_map/bis,bsw->biw/dot_general | solution.py:28
  285.0 39.6 %all-gather.12.cloned.1.call-done = bf16[64,256,256]{2,1,0:T(8,128)(2,1)} async-done(((bf16[4,256,256]{2,1,0:T(8,128)(2,1)}), bf16[64,256,256]{2,1,0:T(8,128)(2,1)}) %all-gather.12.cloned.1.call-update) | async-done | bytes 8388624 | tf_op jit(solution)/shard_map/all_gather | solution.py:53
  324.6 5.6 %multiply_reduce_fusion = f32[64,256]{1,0:T(8,128)S(1)} fusion(bf16[64,256,256]{2,1,0:T(8,128)(2,1)} %all-gather.12.cloned.1.call-done), kind=kLoop, calls=%fused_computation.33 | loop fusion | flops 12566528 | bytes 8454144 | tf_op jit(solution)/shard_map/reduce_sum | solution.py:16
  331.0 11.9 %gather_fusion.2 = bf16[128,256,256]{2,1,0:T(8,128)(2,1)} fusion(bf16[64,256,256]{2,1,0:T(8,128)(2,1)} %all-gather.12.cloned.1.call-done, s32[1024]{0:T(1024)S(1)} %pad_clamp_fusion.4), kind=kCustom, calls=%fused_computation.2 | custom fusion | bytes 33554944 | tf_op jit(solution)/shard_map/gather | solution.py:81
  342.8 15.7 %add_add_fusion = f32[128,128,64]{1,2,0:T(8,128)} fusion(f32[128,128,64]{1,2,0:T(8,128)} %fusion.16, f32[128,128,64]{1,2,0:T(8,128)} %fusion.17, bf16[128,256,64]{1,2,0:T(8,128)(2,1)} %gather_fusion.3, bf16[128,256,256]{2,1,0:T(8,128)(2,1)} %gather_fusion.2, bf16[128,128,256]{2,1,0:T(8,128)(2,1)} %bitcast.127, f32[128,256]{1,0:T(8,128)S(1)} %gather_fusion.1, ...), kind=kOutput, calls=%fused_computation.62 | convolution fusion | flops 2711617536 | bytes 42139776 | tf_op jit(solution)/shard_map/bis,bsw->biw/dot_general | solution.py:28
  358.6 6.6 %copy.23 = f32[128,128,64]{1,0,2:T(8,128)} copy(f32[128,128,64]{1,2,0:T(8,128)} %add_add_fusion) | data formatting | bytes 8388608 | tf_op jit(solution)/shard_map/add | solution.py:85
  375.6 7.1 %copy.25 = bf16[256,128,64]{1,0,2:T(8,128)(2,1)} copy(bf16[256,128,64]{1,2,0:T(8,128)(2,1)} %gather_fusion.12) | data formatting | bytes 8388608 | tf_op jit(solution)/shard_map/gather | solution.py:63
  382.8 7.9 %reshape.307 = bf16[16,2048,64]{1,0,2:T(8,128)(2,1)} reshape(bf16[256,128,64]{1,0,2:T(8,128)(2,1)} %copy.25) | data formatting | bytes 8388608 | tf_op jit(solution)/shard_map/reshape | solution.py:63
  391.4 13.0 %gather_fusion.11 = bf16[256,128,256]{2,1,0:T(8,128)(2,1)} fusion(bf16[128,128,256]{2,1,0:T(8,128)(2,1)} %bitcast.128, s32[1024]{0:T(1024)S(1)} %pad_clamp_fusion.1), kind=kCustom, calls=%fused_computation.11 | custom fusion | bytes 33555456 | tf_op jit(solution)/shard_map/gather | solution.py:61
  404.4 12.3 %fusion.87 = bf16[16,128,2048]{1,2,0:T(8,128)(2,1)S(1)} fusion(f32[16,2048]{1,0:T(8,128)S(1)} %add.223, f32[16,128]{1,0:T(8,128)S(1)} %constant_dynamic-slice_fusion, pred[16,2048]{1,0:T(8,128)(4,1)S(1)} %bitcast.139, bf16[16,2048,256]{2,1,0:T(8,128)(2,1)} %bitcast.135, bf16[16,128,256]{2,1,0:T(8,128)(2,1)S(1)} %bitcast.129), kind=kOutput, calls=%fused_computation.17.clone.clone.clone.clone.1 | convolution fusion | flops 2172649472 | bytes 26386432 | tf_op jit(solution)/shard_map/bie,bse->bis/dot_general | solution.py:20
  416.7 5.0 fusion.43
  421.8 103.9 %all-gather.20.cloned.1.call-done = f32[8,16384,64]{1,2,0:T(8,128)} async-done(((f32[1,16384,64]{1,2,0:T(8,128)}), f32[8,16384,64]{1,2,0:T(8,128)}) %all-gather.20.cloned.1.call-update) | async-done | bytes 33554448 | tf_op jit(solution)/shard_map/all_gather | solution.py:86
  525.7 14.0 %reduce_sum.49 = f32[16384,64]{0,1:T(8,128)} reduce(f32[8,16384,64]{1,2,0:T(8,128)} %all-gather.20.cloned.1.call-done, f32[]{:T(128)} %constant.90.clone.1), dimensions={0}, to_apply=%region_4.5 | reduce | flops 7340032 | bytes 37748740 | tf_op jit(solution)/shard_map/reduce_sum | solution.py:86
  (68 shorter events, 38.3 us)
Async XLA Ops:
  6.5 9.7 %copy-start.3 = (bf16[7,256,64]{1,2,0:T(8,128)(2,1)S(1)}, bf16[7,256,64]{1,2,0:T(8,128)(2,1)}, u32[]{:S(2)}) copy-start(bf16[7,256,64]{1,2,0:T(8,128)(2,1)} %param.11) | copy-start | bytes 688132
  6.5 13.6 %slice-start = ((bf16[7,256,64]{1,2,0:T(8,128)(2,1)}), bf16[1,256,64]{1,2,0:T(8,128)(2,1)S(1)}, s32[]{:S(2)}) async-start(bf16[7,256,64]{1,2,0:T(8,128)(2,1)} %param.11), calls=%async_computation.8 | async-start | bytes 65536 | tf_op jit(solution)/shard_map/slice | solution.py:54
  6.5 13.5 %copy-start.5 = (s32[128,3,1]{0,2,1:T(1,128)S(1)}, s32[128,3,1]{0,2,1:T(1,128)}, u32[]{:S(2)}) copy-start(s32[128,3,1]{0,2,1:T(1,128)} %param.9) | copy-start | bytes 4612
  6.5 48.3 %all-gather.18.cloned.1.call-start = ((), (), s32[]{:S(2)}) async-start(), calls=%async_computation.4 | async-start | bytes 1114112 | tf_op jit(solution)/shard_map/all_gather | solution.py:54
  8.1 93.3 %all-gather.24.cloned.1.call-start = ((), (), s32[]{:S(2)}) async-start(), calls=%async_computation.7 | async-start | bytes 2228224 | tf_op jit(solution)/shard_map/all_gather | solution.py:53
  16.2 131.7 %all-gather.14.cloned.1.call-start = ((), (), s32[]{:S(2)}) async-start(), calls=%async_computation.2 | async-start | bytes 2228224 | tf_op jit(solution)/shard_map/all_gather | solution.py:54
  16.9 183.7 %all-gather.16.cloned.1.call-start = ((), (), s32[]{:S(2)}) async-start(), calls=%async_computation.3 | async-start | bytes 4456448 | tf_op jit(solution)/shard_map/all_gather | solution.py:53
  17.7 233.7 %all-gather.10.cloned.1.call-start = ((), (), s32[]{:S(2)}) async-start(), calls=%async_computation | async-start | bytes 9437184 | tf_op jit(solution)/shard_map/all_gather | solution.py:41
  18.3 306.2 %all-gather.12.cloned.1.call-start = ((), (), s32[]{:S(2)}) async-start(), calls=%async_computation.1 | async-start | bytes 8912896 | tf_op jit(solution)/shard_map/all_gather | solution.py:53
  19.2 351.1 %all-gather.22.cloned.1.call-start = ((), (), s32[]{:S(2)}) async-start(), calls=%async_computation.6 | async-start | bytes 2359296 | tf_op jit(solution)/shard_map/all_gather | solution.py:42
  20.0 505.7 %all-gather.20.cloned.1.call-start = ((), (), s32[]{:S(2)}) async-start(), calls=%async_computation.5 | async-start | bytes 37748736 | tf_op jit(solution)/shard_map/all_gather | solution.py:86
  101.4 10.2 %copy-start = (bf16[4096,256]{1,0:T(8,128)(2,1)S(1)}, bf16[4096,256]{1,0:T(8,128)(2,1)}, u32[]{:S(2)}) copy-start(bf16[4096,256]{1,0:T(8,128)(2,1)} %all-gather.24.cloned.1.call-done) | copy-start | bytes 6291460
  365.1 5.0 copy-start.4
  391.4 13.1 %copy-start.1 = (bf16[2048,256]{1,0:T(8,128)(2,1)S(1)}, bf16[2048,256]{1,0:T(8,128)(2,1)}, u32[]{:S(2)}) copy-start(bf16[2048,256]{1,0:T(8,128)(2,1)} %param.6) | copy-start | bytes 3145732
  404.4 12.3 %copy-start.2 = (bf16[16,2048,64]{1,0,2:T(8,128)(2,1)S(1)}, bf16[16,2048,64]{1,0,2:T(8,128)(2,1)}, u32[]{:S(2)}) copy-start(bf16[16,2048,64]{1,0,2:T(8,128)(2,1)} %reshape.307) | copy-start | bytes 12582916
Sparse Core Ops, SparseCore 0:
  9.5 45.3 all-gather.17
  57.0 44.3 all-gather.23
  103.5 44.2 all-gather.13
  149.8 50.7 all-gather.15
  202.2 49.2 all-gather.9
  253.4 71.0 all-gather.11
  326.3 24.8 all-gather.21
  370.2 155.3 all-gather.19
